TPU v7x, 32 devices: a whole 2x2x4 slice. The times are simulated.
32 devices in a mesh: groups: 2 (over y), row: 4 (over z), col: 2 (over x), rep: 2 (over core).
Axes of the slice: x: 2, y: 2, z: 4, core: 2. Of those that a mesh axis runs over, the one named last changes fastest.
Arguments:
- kernel: float32 [32768, 16384], P(('groups', 'row'), ('col', 'rep')), parts along dimension 0, may hold values from 0 to 2, as said below
- source: float32 [64, 16384], P('groups', 'row'), parts along dimension 0, may hold values from 0.5 to 2, as said below
- target: float32 [64, 16384], P('groups', ('col', 'rep')), parts along dimension 0, may hold values from 0.5 to 2, as said below
Outputs:
- left_scale: float32 [64, 16384], P('groups', 'row'), parts along dimension 0
- right_scale: float32 [64, 16384], P('groups', ('col', 'rep')), parts along dimension 0
- errors: float32 [6, 32], P('groups'), parts along dimension 0
There are 2 independent parts, one for each index of `groups`. A program takes and returns all parts, laid end to end along the dimension named above; each array names one. Nothing has to cross between parts.
Inputs may be any that keep to these rules, and one draw needn't show every extreme that they name: `kernel`: every entry is positive. `source`: every entry is positive. `target`: every entry is positive.
All inputs are finite; a program needn't handle non-finite values.
Results may differ from a plain program's by a relative error of at most 0.0001.
Values sent between devices are 32-bit elements; how exact they have to be, the bound alone decides.
A program may use at most 128 MiB of HBM per device.

v0:
```python
import jax
import jax.numpy as jnp
from jax import lax
from jax.sharding import PartitionSpec as P

N = 16384
ITERS = 3


def local(kernel, source, target):
    columns = kernel.shape[1]
    right_scale = jnp.ones(target.shape, jnp.float32)
    left_scale = source
    share = columns // lax.axis_size("row")
    offset = lax.axis_index("row") * share
    errors = []
    for step in range(ITERS):
        partial_value = lax.dot_general(
            right_scale, kernel, (((1,), (1,)), ((), ())), precision=lax.Precision.HIGHEST
        )
        left_scale = source / lax.psum(partial_value, ("col", "rep"))
        back = jnp.dot(left_scale, kernel, precision=lax.Precision.HIGHEST)
        old_piece = lax.dynamic_slice_in_dim(right_scale, offset, share, 1)
        target_piece = lax.dynamic_slice_in_dim(target, offset, share, 1)
        total_piece = lax.psum_scatter(back, "row", scatter_dimension=1, tiled=True)
        right_scale = lax.all_gather(target_piece / total_piece, "row", axis=1, tiled=True)
        term = jnp.sum(jnp.abs(old_piece * total_piece - target_piece), axis=1) / N
        errors.append(lax.psum(term, ("row", "col", "rep")))
    stacked = jnp.stack(errors)
    return (left_scale, right_scale, stacked)


def solution(mesh):
    return jax.shard_map(
        local,
        mesh=mesh,
        in_specs=(
            P(("groups", "row"), ("col", "rep")),
            P("groups", "row"),
            P("groups", ("col", "rep")),
        ),
        out_specs=(P("groups", "row"), P("groups", ("col", "rep")), P("groups", None)),
        check_vma=False,
    )
```

profile of v0, /device:TPU:0, one launch (start us, length us, event | category | flops | bytes accessed | tf_op | source)
XLA Modules:
  0.0 597.1 jit_solution(12538912805392526422)
XLA Ops:
  7.2 0.0 copy-start
  7.2 0.0 all-reduce.5.cloned.1.call-start
  7.2 66.4 %fusion.4 = f32[32,4096]{1,0:T(8,128)} fusion(f32[4096,4096]{1,0:T(8,128)} %param.3), kind=kOutput, calls=%fused_computation.4 | convolution fusion | flops 6442450944 | bytes 67633152 | tf_op jit(solution)/shard_map/dot_general | solution.py:18
  73.7 0.0 copy-start.4
  73.7 0.0 all-reduce.5.cloned.1.call-update
  73.7 0.3 reduce-scatter.4.cloned.1.call-start
  74.0 36.0 %all-reduce.5.cloned.1.call-done = f32[32,4096]{1,0:T(8,128)} async-done(((f32[32,4096]{1,0:T(8,128)}), f32[32,4096]{1,0:T(8,128)}) %all-reduce.5.cloned.1.call-update) | async-done | bytes 524304 | tf_op jit(solution)/shard_map/psum | solution.py:21
  110.0 0.0 copy-done
  110.0 44.8 %fusion.2 = f32[32,4096]{1,0:T(8,128)} fusion(f32[4096,4096]{1,0:T(8,128)} %param.3, f32[32,4096]{1,0:T(8,128)S(1)} %copy-done, f32[32,4096]{1,0:T(8,128)} %all-reduce.5.cloned.1.call-done), kind=kOutput, calls=%fused_computation.2 | convolution fusion | flops 6442582016 | bytes 68681728 | tf_op jit(solution)/shard_map/dot_general | solution.py:22
  154.8 0.0 reduce-scatter.4.cloned.1.call-update
  154.9 0.0 all-reduce.7.cloned.1.call-start
  154.9 22.1 %reduce-scatter.4.cloned.1.call-done = f32[32,1024]{1,0:T(8,128)} async-done(((f32[32,4096]{1,0:T(8,128)}), f32[32,1024]{1,0:T(8,128)}) %reduce-scatter.4.cloned.1.call-update) | async-done | bytes 131088 | tf_op jit(solution)/shard_map/reduce_scatter | solution.py:25
  177.0 0.0 copy-done.4
  177.0 0.9 dynamic-slice_divide_fusion.2
  177.9 15.7 %all_gather.9 = f32[32,4096]{1,0:T(8,128)S(1)} all-gather(f32[32,1024]{1,0:T(8,128)S(1)} %dynamic-slice_divide_fusion.2), channel_id=1, replica_groups=mesh['groups'=2,'row'=4,'col'=2,'rep'=2] {'row'}, dimensions={1}, use_global_device_ids=true | all-gather | bytes 655360 | tf_op jit(solution)/shard_map/all_gather | solution.py:26
  193.7 66.5 %fusion.7 = f32[32,4096]{1,0:T(8,128)} fusion(f32[32,4096]{1,0:T(8,128)S(1)} %all_gather.9, f32[4096,4096]{1,0:T(8,128)} %param.3), kind=kOutput, calls=%fused_computation.17 | convolution fusion | flops 6442450944 | bytes 68157440 | tf_op jit(solution)/shard_map/dot_general | solution.py:18
  260.2 0.0 all-reduce.7.cloned.1.call-update
  260.2 0.2 reduce-scatter.6.cloned.1.call-start
  260.4 31.8 %all-reduce.7.cloned.1.call-done = f32[32,4096]{1,0:T(8,128)} async-done(((f32[32,4096]{1,0:T(8,128)}), f32[32,4096]{1,0:T(8,128)}) %all-reduce.7.cloned.1.call-update) | async-done | bytes 524304 | tf_op jit(solution)/shard_map/psum | solution.py:21
  292.2 44.8 %fusion = f32[32,4096]{1,0:T(8,128)} fusion(f32[4096,4096]{1,0:T(8,128)} %param.3, f32[32,4096]{1,0:T(8,128)S(1)} %copy-done, f32[32,4096]{1,0:T(8,128)} %all-reduce.7.cloned.1.call-done), kind=kOutput, calls=%fused_computation | convolution fusion | flops 6442582016 | bytes 68681728 | tf_op jit(solution)/shard_map/dot_general | solution.py:22
  337.0 0.0 reduce-scatter.6.cloned.1.call-update
  337.0 0.0 all-reduce.9.cloned.1.call-start
  337.1 22.0 %reduce-scatter.6.cloned.1.call-done = f32[32,1024]{1,0:T(8,128)} async-done(((f32[32,4096]{1,0:T(8,128)}), f32[32,1024]{1,0:T(8,128)}) %reduce-scatter.6.cloned.1.call-update) | async-done | bytes 131088 | tf_op jit(solution)/shard_map/reduce_scatter | solution.py:25
  359.1 0.9 dynamic-slice_divide_fusion.1
  360.0 15.7 %all_gather.10 = f32[32,4096]{1,0:T(8,128)S(1)} all-gather(f32[32,1024]{1,0:T(8,128)S(1)} %dynamic-slice_divide_fusion.1), channel_id=1, replica_groups=mesh['groups'=2,'row'=4,'col'=2,'rep'=2] {'row'}, dimensions={1}, use_global_device_ids=true | all-gather | bytes 655360 | tf_op jit(solution)/shard_map/all_gather | solution.py:26
  375.7 66.5 %fusion.8 = f32[32,4096]{1,0:T(8,128)} fusion(f32[32,4096]{1,0:T(8,128)S(1)} %all_gather.10, f32[4096,4096]{1,0:T(8,128)} %param.3), kind=kOutput, calls=%fused_computation.18 | convolution fusion | flops 6442450944 | bytes 68157440 | tf_op jit(solution)/shard_map/dot_general | solution.py:18
  442.2 0.0 copy-start.2
  442.2 0.0 copy-start.3
  442.2 0.0 all-reduce.9.cloned.1.call-update
  442.2 0.3 reduce-scatter.8.cloned.1.call-start
  442.5 31.6 %all-reduce.9.cloned.1.call-done = f32[32,4096]{1,0:T(8,128)} async-done(((f32[32,4096]{1,0:T(8,128)}), f32[32,4096]{1,0:T(8,128)}) %all-reduce.9.cloned.1.call-update) | async-done | bytes 524304 | tf_op jit(solution)/shard_map/psum | solution.py:21
  474.2 1.1 div.31
  475.3 0.0 copy-start.1
  475.3 45.0 %fusion.9 = f32[32,4096]{1,0:T(8,128)} fusion(f32[32,4096]{1,0:T(8,128)S(1)} %div.31, f32[4096,4096]{1,0:T(8,128)} %param.3), kind=kOutput, calls=%fused_computation.19 | convolution fusion | flops 6442450944 | bytes 68157440 | tf_op jit(solution)/shard_map/dot_general | solution.py:22
  520.3 0.0 reduce-scatter.8.cloned.1.call-update
  520.4 22.1 %reduce-scatter.8.cloned.1.call-done = f32[32,1024]{1,0:T(8,128)} async-done(((f32[32,4096]{1,0:T(8,128)}), f32[32,1024]{1,0:T(8,128)}) %reduce-scatter.8.cloned.1.call-update) | async-done | bytes 131088 | tf_op jit(solution)/shard_map/reduce_scatter | solution.py:25
  542.5 0.0 copy-done.2
  542.5 0.0 copy-done.3
  542.5 1.1 abs_reduce_fusion.2
  543.6 15.3 %all_gather.11 = f32[32,4096]{1,0:T(8,128)S(1)} all-gather(f32[32,1024]{1,0:T(8,128)S(1)} %get-tuple-element.9), channel_id=1, replica_groups=mesh['groups'=2,'row'=4,'col'=2,'rep'=2] {'row'}, dimensions={1}, use_global_device_ids=true | all-gather | bytes 655360 | tf_op jit(solution)/shard_map/all_gather | solution.py:26
  558.9 29.5 %all-reduce = (f32[1,32]{1,0:T(1,128)S(1)}, f32[1,32]{1,0:T(1,128)S(1)}, f32[1,32]{1,0:T(1,128)S(1)}) all-reduce(f32[1,32]{1,0:T(1,128)S(1)} %get-tuple-element.10, f32[1,32]{1,0:T(1,128)S(1)} %get-tuple-element.11, f32[1,32]{1,0:T(1,128)S(1)} %multiply_bitcast_fusion.2), channel_id=1, replica_groups=mesh['groups'=2,'row'=4,'col'=2,'rep'=2] {'row','col','rep'}, use_global_device_ids=true, to_apply=%region_11.0 | all-reduce | flops 96 | bytes 768 | tf_op jit(solution)/shard_map/psum | solution.py:28
  588.4 0.6 pad_maximum_fusion
  589.0 0.8 copy.10
  589.8 0.0 copy-done.1
  (2 shorter events, 0.0 us)
Async XLA Ops:
  7.2 102.8 %copy-start = (f32[32,4096]{1,0:T(8,128)S(1)}, f32[32,4096]{1,0:T(8,128)}, u32[]{:S(2)}) copy-start(f32[32,4096]{1,0:T(8,128)} %param.4) | copy-start | bytes 1572868
  7.2 102.8 %all-reduce.5.cloned.1.call-start = ((), (), s32[]{:S(2)}) async-start(), calls=%async_computation.3 | async-start | bytes 1048576 | tf_op jit(solution)/shard_map/psum | solution.py:21
  73.7 103.3 %copy-start.4 = (f32[32,4096]{1,0:T(8,128)S(1)}, f32[32,4096]{1,0:T(8,128)}, u32[]{:S(2)}) copy-start(f32[32,4096]{1,0:T(8,128)} %param.5) | copy-start | bytes 1572868
  73.7 103.3 %reduce-scatter.4.cloned.1.call-start = ((), (), s32[]{:S(2)}) async-start(), calls=%async_computation.4 | async-start | bytes 655360 | tf_op jit(solution)/shard_map/reduce_scatter | solution.py:25
  154.9 137.3 %all-reduce.7.cloned.1.call-start = ((), (), s32[]{:S(2)}) async-start(), calls=%async_computation.5 | async-start | bytes 1048576 | tf_op jit(solution)/shard_map/psum | solution.py:21
  260.2 98.9 %reduce-scatter.6.cloned.1.call-start = ((), (), s32[]{:S(2)}) async-start(), calls=%async_computation.6 | async-start | bytes 655360 | tf_op jit(solution)/shard_map/reduce_scatter | solution.py:25
  337.0 137.1 %all-reduce.9.cloned.1.call-start = ((), (), s32[]{:S(2)}) async-start(), calls=%async_computation.7 | async-start | bytes 1048576 | tf_op jit(solution)/shard_map/psum | solution.py:21
  442.2 100.3 %copy-start.2 = (f32[32,1024]{1,0:T(8,128)S(1)}, f32[32,1024]{1,0:T(8,128)}, u32[]{:S(2)}) copy-start(f32[32,1024]{1,0:T(8,128)} %reduce-scatter.4.cloned.1.call-done) | copy-start | bytes 393220
  442.2 100.3 %copy-start.3 = (f32[32,1024]{1,0:T(8,128)S(1)}, f32[32,1024]{1,0:T(8,128)}, u32[]{:S(2)}) copy-start(f32[32,1024]{1,0:T(8,128)} %reduce-scatter.6.cloned.1.call-done) | copy-start | bytes 393220
  442.2 100.2 %reduce-scatter.8.cloned.1.call-start = ((), (), s32[]{:S(2)}) async-start(), calls=%async_computation.8 | async-start | bytes 655360 | tf_op jit(solution)/shard_map/reduce_scatter | solution.py:25
  475.3 114.5 %copy-start.1 = (f32[32,4096]{1,0:T(8,128)}, f32[32,4096]{1,0:T(8,128)S(1)}, u32[]{:S(2)}) copy-start(f32[32,4096]{1,0:T(8,128)S(1)} %div.31) | copy-start | bytes 1572868
Sparse Core Ops, SparseCore 0:
  73.8 36.1 all-reduce.4
  155.0 21.9 reduce-scatter.3
  260.3 31.8 all-reduce.6
  337.1 21.9 reduce-scatter.5
  442.4 31.7 all-reduce.8
  520.5 21.9 reduce-scatter.7
where the time goes:
time: 606 us; the launch traced here: 597 us
  matrix products  334 us (55%)
  waiting for transfers between devices  166 us (27%)
  blocking collectives  76.2 us (13%)
  between operations  14.6 us (2%)
    dot_general x3, matrix products, local(): lax.dot_general(right_scale, kernel, (((1,), (1,)), ((), ())), precision=...  199 us
    dot_general x3, matrix products, local(): back = jnp.dot(left_scale, kernel, precision=lax.Precision.HIGHEST)  135 us
    psum x3, waiting for transfers between devices, local(): left_scale = source / lax.psum(partial_value, ('col', 'rep'))  99.4 us
    reduce_scatter x3, waiting for transfers between devices, local(): total_piece = lax.psum_scatter(back, 'row', scatter_dimension=1, tiled=True)  66.2 us
    all_gather x3, blocking collectives, local(): lax.all_gather(target_piece / total_piece, 'row', axis=1, tiled=True)  46.8 us
    psum x1, blocking collectives, local(): errors.append(lax.psum(term, ('row', 'col', 'rep')))  29.5 us
  transfers between devices with their start and end apart: 6, of which 6 were waited for; matrix products, arithmetic and copies ran while one was open for 0% of the time, Pallas kernels for 0%

commit v1 on v0

--- a/solution.py
+++ b/solution.py
@@ -18,7 +18,7 @@
         partial_value = lax.dot_general(
             right_scale, kernel, (((1,), (1,)), ((), ())), precision=lax.Precision.HIGHEST
         )
-        left_scale = source / lax.psum(partial_value, ("col", "rep"))
+        left_scale = source / jnp.sum(lax.all_gather(partial_value, ("col", "rep")), axis=0)
         back = jnp.dot(left_scale, kernel, precision=lax.Precision.HIGHEST)
         old_piece = lax.dynamic_slice_in_dim(right_scale, offset, share, 1)
         target_piece = lax.dynamic_slice_in_dim(target, offset, share, 1)

time: 606 us -> 577 us (0.952)
  waiting for transfers between devices: 166 us -> 133 us
    psum x3 -> x0, waiting for transfers between devices: 99.4 us -> none  [local(): left_scale = source / lax.psum(partial_value, ('col', 'rep'))]
    all_gather x0 -> x3, waiting for transfers between devices: none -> 67 us  [local(): lax.all_gather(partial_value, ('col', 'rep'))]
where the time goes in v1:
time: 577 us; the launch traced here: 568 us
  matrix products  334 us (58%)
  waiting for transfers between devices  133 us (23%)
  blocking collectives  76.2 us (13%)
  between operations  14.6 us (3%)
  other arithmetic  8.91 us (2%)
    dot_general x3, matrix products, local(): lax.dot_general(right_scale, kernel, (((1,), (1,)), ((), ())), precision=...  199 us
    dot_general x3, matrix products, local(): back = jnp.dot(left_scale, kernel, precision=lax.Precision.HIGHEST)  135 us
    all_gather x3, waiting for transfers between devices, local(): lax.all_gather(partial_value, ('col', 'rep'))  67 us
    reduce_scatter x3, waiting for transfers between devices, local(): total_piece = lax.psum_scatter(back, 'row', scatter_dimension=1, tiled=True)  65.8 us
    all_gather x3, blocking collectives, local(): lax.all_gather(target_piece / total_piece, 'row', axis=1, tiled=True)  46.7 us
    psum x1, blocking collectives, local(): errors.append(lax.psum(term, ('row', 'col', 'rep')))  29.5 us
  transfers between devices with their start and end apart: 6, of which 6 were waited for; matrix products, arithmetic and copies ran while one was open for 0% of the time, Pallas kernels for 0%

profile of v1, /device:TPU:0, one launch (start us, length us, event | category | flops | bytes accessed | tf_op | source)
XLA Modules:
  0.0 568.4 jit_solution(2878039164460441787)
XLA Ops:
  7.2 0.0 copy-start
  7.2 0.0 all-gather.7.cloned.1.call-start
  7.2 66.4 %fusion.4 = f32[32,4096]{1,0:T(8,128)} fusion(f32[4096,4096]{1,0:T(8,128)} %param.3), kind=kOutput, calls=%fused_computation.4 | convolution fusion | flops 6442450944 | bytes 67633152 | tf_op jit(solution)/shard_map/dot_general | solution.py:18
  73.7 0.0 copy-start.4
  73.7 0.0 all-gather.7.cloned.1.call-update
  73.7 0.3 reduce-scatter.4.cloned.1.call-start
  74.0 25.2 %all-gather.7.cloned.1.call-done = f32[128,4096]{1,0:T(8,128)} async-done(((f32[32,4096]{1,0:T(8,128)}), f32[128,4096]{1,0:T(8,128)}) %all-gather.7.cloned.1.call-update) | async-done | bytes 2097168 | tf_op jit(solution)/shard_map/all_gather | solution.py:21
  99.1 1.8 reduce_sum.54
  100.9 0.0 copy-done
  100.9 44.8 %fusion.2 = f32[32,4096]{1,0:T(8,128)} fusion(f32[4096,4096]{1,0:T(8,128)} %param.3, f32[32,4096]{1,0:T(8,128)S(1)} %copy-done, f32[32,4096]{1,0:T(8,128)S(1)} %reduce_sum.54), kind=kOutput, calls=%fused_computation.2 | convolution fusion | flops 6442582016 | bytes 68681728 | tf_op jit(solution)/shard_map/dot_general | solution.py:22
  145.7 0.0 reduce-scatter.4.cloned.1.call-update
  145.7 0.0 all-gather.9.cloned.1.call-start
  145.8 21.9 %reduce-scatter.4.cloned.1.call-done = f32[32,1024]{1,0:T(8,128)} async-done(((f32[32,4096]{1,0:T(8,128)}), f32[32,1024]{1,0:T(8,128)}) %reduce-scatter.4.cloned.1.call-update) | async-done | bytes 131088 | tf_op jit(solution)/shard_map/reduce_scatter | solution.py:25
  167.7 0.0 copy-done.4
  167.7 0.9 dynamic-slice_divide_fusion.2
  168.6 15.8 %all_gather.29 = f32[32,4096]{1,0:T(8,128)S(1)} all-gather(f32[32,1024]{1,0:T(8,128)S(1)} %dynamic-slice_divide_fusion.2), channel_id=1, replica_groups=mesh['groups'=2,'row'=4,'col'=2,'rep'=2] {'row'}, dimensions={1}, use_global_device_ids=true | all-gather | bytes 655360 | tf_op jit(solution)/shard_map/all_gather | solution.py:26
  184.4 66.5 %fusion.7 = f32[32,4096]{1,0:T(8,128)} fusion(f32[32,4096]{1,0:T(8,128)S(1)} %all_gather.29, f32[4096,4096]{1,0:T(8,128)} %param.3), kind=kOutput, calls=%fused_computation.17 | convolution fusion | flops 6442450944 | bytes 68157440 | tf_op jit(solution)/shard_map/dot_general | solution.py:18
  250.9 0.0 all-gather.9.cloned.1.call-update
  250.9 0.2 reduce-scatter.6.cloned.1.call-start
  251.1 21.0 %all-gather.9.cloned.1.call-done = f32[128,4096]{1,0:T(8,128)} async-done(((f32[32,4096]{1,0:T(8,128)}), f32[128,4096]{1,0:T(8,128)}) %all-gather.9.cloned.1.call-update) | async-done | bytes 2097168 | tf_op jit(solution)/shard_map/all_gather | solution.py:21
  272.1 1.8 reduce_sum.55
  273.8 44.8 %fusion = f32[32,4096]{1,0:T(8,128)} fusion(f32[4096,4096]{1,0:T(8,128)} %param.3, f32[32,4096]{1,0:T(8,128)S(1)} %copy-done, f32[32,4096]{1,0:T(8,128)S(1)} %reduce_sum.55), kind=kOutput, calls=%fused_computation | convolution fusion | flops 6442582016 | bytes 68681728 | tf_op jit(solution)/shard_map/dot_general | solution.py:22
  318.6 0.0 reduce-scatter.6.cloned.1.call-update
  318.7 0.0 all-gather.11.cloned.1.call-start
  318.7 21.9 %reduce-scatter.6.cloned.1.call-done = f32[32,1024]{1,0:T(8,128)} async-done(((f32[32,4096]{1,0:T(8,128)}), f32[32,1024]{1,0:T(8,128)}) %reduce-scatter.6.cloned.1.call-update) | async-done | bytes 131088 | tf_op jit(solution)/shard_map/reduce_scatter | solution.py:25
  340.6 0.9 dynamic-slice_divide_fusion.1
  341.6 15.6 %all_gather.32 = f32[32,4096]{1,0:T(8,128)S(1)} all-gather(f32[32,1024]{1,0:T(8,128)S(1)} %dynamic-slice_divide_fusion.1), channel_id=1, replica_groups=mesh['groups'=2,'row'=4,'col'=2,'rep'=2] {'row'}, dimensions={1}, use_global_device_ids=true | all-gather | bytes 655360 | tf_op jit(solution)/shard_map/all_gather | solution.py:26
  357.1 66.5 %fusion.8 = f32[32,4096]{1,0:T(8,128)} fusion(f32[32,4096]{1,0:T(8,128)S(1)} %all_gather.32, f32[4096,4096]{1,0:T(8,128)} %param.3), kind=kOutput, calls=%fused_computation.18 | convolution fusion | flops 6442450944 | bytes 68157440 | tf_op jit(solution)/shard_map/dot_general | solution.py:18
  423.6 0.0 copy-start.2
  423.6 0.0 copy-start.3
  423.6 0.0 all-gather.11.cloned.1.call-update
  423.7 0.3 reduce-scatter.8.cloned.1.call-start
  424.0 20.9 %all-gather.11.cloned.1.call-done = f32[128,4096]{1,0:T(8,128)} async-done(((f32[32,4096]{1,0:T(8,128)}), f32[128,4096]{1,0:T(8,128)}) %all-gather.11.cloned.1.call-update) | async-done | bytes 2097168 | tf_op jit(solution)/shard_map/all_gather | solution.py:21
  444.8 1.8 reduce_sum.56
  446.6 0.1 div.31
  446.7 0.0 copy-start.1
  446.7 45.0 %fusion.9 = f32[32,4096]{1,0:T(8,128)} fusion(f32[32,4096]{1,0:T(8,128)S(1)} %div.31, f32[4096,4096]{1,0:T(8,128)} %param.3), kind=kOutput, calls=%fused_computation.19 | convolution fusion | flops 6442450944 | bytes 68157440 | tf_op jit(solution)/shard_map/dot_general | solution.py:22
  491.7 0.0 reduce-scatter.8.cloned.1.call-update
  491.7 22.0 %reduce-scatter.8.cloned.1.call-done = f32[32,1024]{1,0:T(8,128)} async-done(((f32[32,4096]{1,0:T(8,128)}), f32[32,1024]{1,0:T(8,128)}) %reduce-scatter.8.cloned.1.call-update) | async-done | bytes 131088 | tf_op jit(solution)/shard_map/reduce_scatter | solution.py:25
  513.7 0.0 copy-done.2
  513.7 0.0 copy-done.3
  513.7 1.1 abs_reduce_fusion.2
  514.8 15.4 %all_gather.35 = f32[32,4096]{1,0:T(8,128)S(1)} all-gather(f32[32,1024]{1,0:T(8,128)S(1)} %get-tuple-element.9), channel_id=1, replica_groups=mesh['groups'=2,'row'=4,'col'=2,'rep'=2] {'row'}, dimensions={1}, use_global_device_ids=true | all-gather | bytes 655360 | tf_op jit(solution)/shard_map/all_gather | solution.py:26
  530.2 29.5 %all-reduce = (f32[1,32]{1,0:T(1,128)S(1)}, f32[1,32]{1,0:T(1,128)S(1)}, f32[1,32]{1,0:T(1,128)S(1)}) all-reduce(f32[1,32]{1,0:T(1,128)S(1)} %get-tuple-element.10, f32[1,32]{1,0:T(1,128)S(1)} %get-tuple-element.11, f32[1,32]{1,0:T(1,128)S(1)} %multiply_bitcast_fusion.2), channel_id=1, replica_groups=mesh['groups'=2,'row'=4,'col'=2,'rep'=2] {'row','col','rep'}, use_global_device_ids=true, to_apply=%region_11.0 | all-reduce | flops 96 | bytes 768 | tf_op jit(solution)/shard_map/psum | solution.py:28
  559.7 0.6 pad_maximum_fusion
  560.3 0.8 copy.7
  561.1 0.0 copy-done.1
  (2 shorter events, 0.0 us)
Async XLA Ops:
  7.2 93.7 %copy-start = (f32[32,4096]{1,0:T(8,128)S(1)}, f32[32,4096]{1,0:T(8,128)}, u32[]{:S(2)}) copy-start(f32[32,4096]{1,0:T(8,128)} %param.4) | copy-start | bytes 1572868
  7.2 92.0 %all-gather.7.cloned.1.call-start = ((), (), s32[]{:S(2)}) async-start(), calls=%async_computation.6 | async-start | bytes 2621440 | tf_op jit(solution)/shard_map/all_gather | solution.py:21
  73.7 94.0 %copy-start.4 = (f32[32,4096]{1,0:T(8,128)S(1)}, f32[32,4096]{1,0:T(8,128)}, u32[]{:S(2)}) copy-start(f32[32,4096]{1,0:T(8,128)} %param.5) | copy-start | bytes 1572868
  73.7 94.0 %reduce-scatter.4.cloned.1.call-start = ((), (), s32[]{:S(2)}) async-start(), calls=%async_computation.3 | async-start | bytes 655360 | tf_op jit(solution)/shard_map/reduce_scatter | solution.py:25
  145.7 126.4 %all-gather.9.cloned.1.call-start = ((), (), s32[]{:S(2)}) async-start(), calls=%async_computation.7 | async-start | bytes 2621440 | tf_op jit(solution)/shard_map/all_gather | solution.py:21
  250.9 89.7 %reduce-scatter.6.cloned.1.call-start = ((), (), s32[]{:S(2)}) async-start(), calls=%async_computation.4 | async-start | bytes 655360 | tf_op jit(solution)/shard_map/reduce_scatter | solution.py:25
  318.7 126.2 %all-gather.11.cloned.1.call-start = ((), (), s32[]{:S(2)}) async-start(), calls=%async_computation.8 | async-start | bytes 2621440 | tf_op jit(solution)/shard_map/all_gather | solution.py:21
  423.6 90.1 %copy-start.2 = (f32[32,1024]{1,0:T(8,128)S(1)}, f32[32,1024]{1,0:T(8,128)}, u32[]{:S(2)}) copy-start(f32[32,1024]{1,0:T(8,128)} %reduce-scatter.4.cloned.1.call-done) | copy-start | bytes 393220
  423.6 90.1 %copy-start.3 = (f32[32,1024]{1,0:T(8,128)S(1)}, f32[32,1024]{1,0:T(8,128)}, u32[]{:S(2)}) copy-start(f32[32,1024]{1,0:T(8,128)} %reduce-scatter.6.cloned.1.call-done) | copy-start | bytes 393220
  423.7 90.0 %reduce-scatter.8.cloned.1.call-start = ((), (), s32[]{:S(2)}) async-start(), calls=%async_computation.5 | async-start | bytes 655360 | tf_op jit(solution)/shard_map/reduce_scatter | solution.py:25
  446.7 114.4 %copy-start.1 = (f32[32,4096]{1,0:T(8,128)}, f32[32,4096]{1,0:T(8,128)S(1)}, u32[]{:S(2)}) copy-start(f32[32,4096]{1,0:T(8,128)S(1)} %div.31) | copy-start | bytes 1572868
Sparse Core Ops, SparseCore 0:
  73.8 25.2 all-gather.6
  145.8 21.8 reduce-scatter.3
  251.0 21.0 all-gather.8
  318.8 21.8 reduce-scatter.5
  423.8 20.9 all-gather.10
  491.9 21.8 reduce-scatter.7
